TPU v7x, 32 devices: a whole 2x2x4 slice. The times are simulated.
32 devices in a mesh: runs: 2 (over y), amp: 16 (over z, x, core).
Axes of the slice: x: 2, y: 2, z: 4, core: 2. Of those that a mesh axis runs over, the one named last changes fastest.
Arguments:
- initial_state: float32 [256, 128, 128], P(('runs', 'amp')), parts along dimension 0, may hold values from -100 to 100
- gate_angles: float32 [10, 16], P('runs'), parts along dimension 0, may hold values from -3.140625 to 3.140625
- gate_pairs: int32 [5, 16, 2], replicated, may hold values from 0 to 6, as said below
- hop_coef: float32 [23], replicated, may hold values from 0.1 to 0.4
- hop_mask: int32 [23], replicated, may hold values 0 or 1
Outputs:
- adjoint: float32 [256, 128, 128], P(('runs', 'amp')), parts along dimension 0
- block_grads: float32 [10, 128, 128], P('runs'), parts along dimension 0
There are 2 independent parts, one for each index of `runs`. A program takes and returns all parts, laid end to end along the dimension named above; an argument that names none is the same for every part. Nothing has to cross between parts.
Inputs may be any that keep to these rules, and one draw needn't show every extreme that they name: `gate_pairs`: the two qubits of each rotation differ.
All inputs are finite; a program needn't handle non-finite values.
Results may differ from a plain program's by a relative error of at most 0.0003.
Values sent between devices are 32-bit elements; how exact they have to be, the bound alone decides.
A program may use at most 192 MiB of HBM per device.

v0:
```python
import functools
import jax
import jax.numpy as jnp
from jax import lax
from jax.experimental import pallas as pl
from jax.experimental.pallas import tpu as pltpu
from jax.sharding import PartitionSpec as P

YQ = 3
AXIS = "amp"
f32 = jnp.float32
bf16 = jnp.bfloat16
NN = ((1,), (0,))
NT = ((1,), (1,))
TN = ((0,), (0,))


def split(x):
    high = x.astype(bf16)
    return high, (x - high.astype(f32)).astype(bf16)


def dot_of(a, b, dims):
    return lax.dot_general(a, b, (dims, ((), ())), preferred_element_type=f32)


def dot3(a, b, dims=NN):
    ah, al = a if isinstance(a, tuple) else split(a)
    bh, bl = b if isinstance(b, tuple) else split(b)
    return dot_of(ah, bh, dims) + (dot_of(ah, bl, dims) + dot_of(al, bh, dims))


def rows_of(ref, start, size, stride):
    if stride == 1:
        return ref[pl.ds(start, size), :]
    return ref[pl.ds(start, size, stride=stride), :]


def put_rows(ref, start, size, stride, value):
    if stride == 1:
        ref[pl.ds(start, size), :] = value
    else:
        ref[pl.ds(start, size, stride=stride), :] = value


def apply_rows(dst, src, matrix, starts, size, stride):
    halves = split(matrix)
    for start in starts:
        put_rows(dst, start, size, stride, dot3(halves, rows_of(src, start, size, stride)))


def gram_rows(left, right, starts, size, stride, right_stride=None, right_starts=None):
    right_starts = starts if right_starts is None else right_starts
    right_stride = stride if right_stride is None else right_stride
    total = None
    for number in range(0, len(starts), 2):
        pick = range(number, min(number + 2, len(starts)))
        a = jnp.concatenate([rows_of(left, starts[i], size, stride) for i in pick], axis=1)
        b = jnp.concatenate(
            [rows_of(right, right_starts[i], size, right_stride) for i in pick], axis=1
        )
        part = dot3(a, b, NT)
        total = part if total is None else total + part
    return total


def apply_lanes(dst, src, matrix):
    rows = src.shape[0]
    halves = split(matrix)
    step = min(256, rows)
    for start in range(0, rows, step):
        dst[pl.ds(start, step), :] = dot3(src[pl.ds(start, step), :], halves)


def gram_lanes(left, right):
    rows = left.shape[0]
    total = None
    step = min(256, rows)
    for start in range(0, rows, step):
        part = dot3(left[pl.ds(start, step), :], right[pl.ds(start, step), :], TN)
        total = part if total is None else total + part
    return total


def spread_matrix(lanes):
    row = lax.broadcasted_iota(jnp.int32, (4 * lanes, lanes), 0)
    col = lax.broadcasted_iota(jnp.int32, (4 * lanes, lanes), 1)
    return jnp.where(lax.shift_right_logical(row, 2) == col, 1.0, 0.0).astype(bf16)


def same_low(lanes):
    row = lax.broadcasted_iota(jnp.int32, (4 * lanes, 4 * lanes), 0)
    col = lax.broadcasted_iota(jnp.int32, (4 * lanes, 4 * lanes), 1)
    return (row & 3) == (col & 3)


def widen(matrix):
    lanes = matrix.shape[0]
    spread = spread_matrix(lanes)
    keep = same_low(lanes)
    made = []
    for part in split(matrix):
        left = dot_of(spread, part, NN).astype(bf16)
        full = dot_of(left, spread, NT)
        made.append(jnp.where(keep, full, 0.0).astype(bf16))
    return tuple(made)


def quads(ref):
    count = ref.shape[0] // 4
    return jnp.concatenate([ref[pl.ds(q, count, stride=4), :] for q in range(4)], axis=1)


def apply_quads(dst, values, matrix):
    lanes = matrix.shape[0]
    result = dot3(values, widen(matrix))
    count = result.shape[0]
    for q in range(4):
        dst[pl.ds(q, count, stride=4), :] = result[:, q * lanes : (q + 1) * lanes]


def gram_quads(left, right):
    lanes = left[0].shape[1] // 4
    full = jnp.where(same_low(lanes), dot3(left, right, TN), 0.0)
    spread = spread_matrix(lanes)
    fh, fl = split(full)
    half = dot_of(fh, spread, NN) + dot_of(fl, spread, NN)
    hh, hl = split(half)
    return dot_of(spread, hh, TN) + dot_of(spread, hl, TN)


def mid_starts(rows, mid_count, lanes):
    stride = min(2 ** (YQ - 1), mid_count // lanes)
    groups = rows // (stride * lanes)
    return [g * stride * lanes + s for g in range(groups) for s in range(stride)], stride


def front_kernel(mid_count, pairs, x, angles, ut, u, s1, s2, s3):
    blocks, lanes = ut.shape[0], ut.shape[1]
    givens = angles.shape[1]
    cosines = jnp.cos(angles[...])
    sines = jnp.sin(angles[...])
    lane = lax.broadcasted_iota(jnp.int32, (8, lanes), 1)
    row = lax.broadcasted_iota(jnp.int32, (lanes, lanes), 0)
    col = lax.broadcasted_iota(jnp.int32, (lanes, lanes), 1)
    for b in range(blocks):
        ut[b] = jnp.where(row == col, 1.0, 0.0)
    for g in range(givens):
        for b in range(blocks):
            p = pairs[b, g, 0]
            s = pairs[b, g, 1]
            low = lax.shift_right_logical(lane, p) & 1
            high = lax.shift_right_logical(lane, s) & 1
            cosine = jnp.broadcast_to(cosines[b : b + 1, g : g + 1], (8, lanes))
            sine = jnp.broadcast_to(sines[b : b + 1, g : g + 1], (8, lanes))
            keep = jnp.where(low != high, cosine, 1.0)[:1]
            up = jnp.where(low < high, -sine, 0.0)[:1]
            down = jnp.where(low > high, sine, 0.0)[:1]
            gap = lax.shift_left(jnp.int32(1), p) - lax.shift_left(jnp.int32(1), s)
            now = ut[b]
            ut[b] = (
                now * keep
                + pltpu.roll(now, (lanes - gap) & (lanes - 1), 1) * up
                + pltpu.roll(now, (lanes + gap) & (lanes - 1), 1) * down
            )
    for b in range(blocks):
        u[b] = jnp.transpose(ut[b])
    apply_lanes(s1, x, ut[0])
    apply_quads(s2, quads(s1), ut[1])
    starts, stride = mid_starts(x.shape[0], mid_count, lanes)
    apply_rows(s3, s2, u[2], starts, lanes, stride)


def hop_matrix(size, terms):
    row = lax.broadcasted_iota(jnp.int32, (size, size), 0)
    col = lax.broadcasted_iota(jnp.int32, (size, size), 1)
    gap = row ^ col
    total = jnp.zeros((size, size), f32)
    for lower, upper, weight in terms:
        differ = (lax.shift_right_logical(row, lower) & 1) != (
            lax.shift_right_logical(row, upper) & 1
        )
        total = total + jnp.where(differ & (gap == (1 << lower | 1 << upper)), weight, 0.0)
    return total


def flip_matrix(size, bit, side, weight):
    row = lax.broadcasted_iota(jnp.int32, (size, size), 0)
    col = lax.broadcasted_iota(jnp.int32, (size, size), 1)
    active = ((lax.shift_right_logical(row, bit) & 1) != side) & ((row ^ col) == (1 << bit))
    return jnp.where(active, weight, 0.0)


def main_kernel(
    n, mid_count, ranks, coef, mask, s3, s2, s1, s0, ut, u,
    adj, grads,
    xb, s4, yb, zb, rungs, chain, l4, l3, back, l2,
    part_a, part_b, got_a, got_b, sum_a, sum_b, full_a, full_b,
    sem_a, sem_x, sem_b, sem_r,
):
    me = lax.axis_index(AXIS)
    top_local, _, lanes = s3.shape
    top, low, _ = xb.shape
    rows = top * low
    low_bits = low.bit_length() - 1
    top_bits = top.bit_length() - 1
    lane_bits = lanes.bit_length() - 1
    flat = lambda ref: ref.reshape(rows, lanes)
    mid_flat = top_local * mid_count

    def each_peer(body):
        def step(d, carry):
            body(lax.rem(me + d, n))
            return carry
        lax.fori_loop(1, n, step, 0)

    barrier = pltpu.get_barrier_semaphore()
    each_peer(lambda peer: pl.semaphore_signal(barrier, inc=1, device_id={AXIS: peer}))
    pl.semaphore_wait(barrier, n - 1)

    def remote(src, dst, send, recv, peer):
        return pltpu.make_async_remote_copy(
            src_ref=src, dst_ref=dst, send_sem=send, recv_sem=recv, device_id={AXIS: peer}
        )

    def settle(ref, send, recv):
        whole = remote(ref, ref, send, recv, lax.rem(me + 1, n))
        whole.wait_recv()
        whole.wait_send()

    mine_rows = pl.ds(pl.multiple_of(me * top_local, top_local), top_local)
    mine_mid = pl.ds(pl.multiple_of(me * low, low), low)

    each_peer(
        lambda peer: remote(
            s3.at[:, pl.ds(pl.multiple_of(peer * low, low), low), :],
            xb.at[mine_rows], sem_a.at[0], sem_a.at[1], peer,
        ).start()
    )
    xb[mine_rows] = s3[:, mine_mid, :]

    weights = [coef[h] * mask[h].astype(f32) for h in range(coef.shape[0])]
    first_top = lane_bits + YQ
    first_rung = first_top + top_bits - 1
    lane_hops = split(hop_matrix(lanes, [(h, h + 1, weights[h]) for h in range(lane_bits - 1)]))
    top_hops = split(
        hop_matrix(top, [(k, k + 1, weights[first_top + k]) for k in range(top_bits - 1)])
    )
    flips = [
        [split(flip_matrix(top, k, side, weights[first_rung + k])) for side in range(2)]
        for k in range(low_bits)
    ]

    settle(xb.at[pl.ds(0, (n - 1) * top_local)], sem_a.at[0], sem_a.at[1])

    xf, s4f, l4f, l3f = flat(xb), s4, l4, flat(l3)
    near = [a * lanes for a in range(rows // lanes)]
    planes = list(range(low))
    apply_rows(s4f, xf, u[3], near, lanes, 1)
    u4 = split(u[4])
    inner = yb.shape[1:]
    for c in planes:
        yb[c] = dot3(u4, s4f[pl.ds(c, top, stride=low), :]).reshape(inner)

    copies = []
    own_bits = [lax.rem(me // (2**k), 2) for k in range(ranks)]

    def half(ref, k, side):
        where = (slice(None),) * (ranks - k) + (side,)
        return ref.at[where]

    def partner(k):
        return me + (1 - 2 * own_bits[k]) * 2**k

    for k in range(ranks - 1, -1, -1):
        copies.append(
            remote(half(yb, k, 1 - own_bits[k]), rungs.at[k], sem_x.at[0, k], sem_x.at[1, k],
                   partner(k))
        )
    half_low = low // 2
    copies.append(
        remote(
            yb.at[pl.ds((1 - own_bits[0]) * half_low, half_low)], chain,
            sem_x.at[0, ranks], sem_x.at[1, ranks], partner(0),
        )
    )
    for copy in copies:
        copy.start()

    lane = lax.broadcasted_iota(jnp.int32, (top, lanes), 1)
    lane_top = lax.shift_right_logical(lane, lane_bits - 1) & 1
    values = lambda c: yb[c].reshape(top, lanes)
    for c in planes:
        own = split(values(c))
        total = dot3(own, lane_hops) + dot3(top_hops, own)
        for k in range(low_bits):
            total = total + dot3(flips[k][c >> k & 1], values(c ^ 1 << k))
        for k in range(low_bits - 1):
            if (c >> k & 1) != (c >> (k + 1) & 1):
                total = total + weights[lane_bits + k] * values(c ^ 3 << k)
        rolled = pltpu.roll(values(c ^ 1), lanes // 2, 1)
        total = total + jnp.where(lane_top != (c & 1), weights[lane_bits - 1] * rolled, 0.0)
        zb[c] = total.reshape(inner)

    for copy in copies:
        copy.wait()
    for k in range(ranks):
        place = half(zb, k, 1 - own_bits[k])
        place[...] = place[...] + weights[first_rung + low_bits + k] * rungs[k]
    seat = pl.ds((1 - own_bits[0]) * half_low, half_low)
    zb[seat] = zb[seat] + weights[lane_bits + low_bits - 1] * chain[...]

    ut4 = split(ut[4])
    gram = None
    for c in planes:
        lam = split(zb[c].reshape(top, lanes))
        part = dot3(lam, s4f[pl.ds(c, top, stride=low), :], NT)
        gram = part if gram is None else gram + part
        l4f[pl.ds(c, top, stride=low), :] = dot3(ut4, lam)
    part_a[pl.ds(lanes, lanes), :] = gram
    apply_rows(l3f, l4f, ut[3], near, lanes, 1)

    each_peer(
        lambda peer: remote(
            l3.at[pl.ds(pl.multiple_of(peer * top_local, top_local), top_local)],
            back.at[:, mine_mid, :], sem_b.at[0], sem_b.at[1], peer,
        ).start()
    )
    back[:, mine_mid, :] = l3[mine_rows]
    part_a[pl.ds(0, lanes), :] = gram_rows(l4f, xf, near, lanes, 1)

    def scatter(part, got, chunk, number):
        each_peer(
            lambda peer: remote(
                part.at[pl.ds(pl.multiple_of(peer * chunk, 8), chunk)], got.at[me],
                sem_r.at[0, number], sem_r.at[1, number], peer,
            ).start()
        )
        got[me] = part[pl.ds(pl.multiple_of(me * chunk, 8), chunk), :]

    factor = 2.0 / (top * mid_count)

    def combine(part, got, mine, full, chunk, number):
        settle(got.at[pl.ds(0, n - 1)], sem_r.at[0, number], sem_r.at[1, number])
        mine[...] = factor * jnp.sum(got[...], axis=0)
        spot = pl.ds(pl.multiple_of(me * chunk, 8), chunk)
        each_peer(
            lambda peer: remote(
                mine, full.at[spot], sem_r.at[0, number + 1], sem_r.at[1, number + 1], peer
            ).start()
        )
        full[spot, :] = mine[...]

    def finish(full, chunk, number):
        settle(full.at[pl.ds(0, (n - 1) * chunk)], sem_r.at[0, number + 1], sem_r.at[1, number + 1])

    chunk_a = sum_a.shape[0]
    chunk_b = sum_b.shape[0]
    if n * chunk_a > 2 * lanes:
        part_a[pl.ds(2 * lanes, n * chunk_a - 2 * lanes), :] = jnp.zeros(
            (n * chunk_a - 2 * lanes, lanes), f32
        )
    if n * chunk_b > 3 * lanes:
        part_b[pl.ds(3 * lanes, n * chunk_b - 3 * lanes), :] = jnp.zeros(
            (n * chunk_b - 3 * lanes, lanes), f32
        )
    scatter(part_a, got_a, chunk_a, 0)

    low_part = pl.ds(0, (n - 1) * low)
    settle(back.at[:, low_part, :], sem_b.at[0], sem_b.at[1])
    backf = back.reshape(mid_flat, lanes)
    starts, stride = mid_starts(mid_flat, mid_count, lanes)
    part_b[pl.ds(2 * lanes, lanes), :] = gram_rows(backf, s2, starts, lanes, stride)
    apply_rows(l2, backf, ut[2], starts, lanes, stride)
    combine(part_a, got_a, sum_a, full_a, chunk_a, 0)
    wide = split(quads(l2))
    part_b[pl.ds(lanes, lanes), :] = gram_quads(wide, split(quads(s1)))
    apply_quads(l2, wide, u[1])
    part_b[pl.ds(0, lanes), :] = gram_lanes(l2, s0)
    scatter(part_b, got_b, chunk_b, 2)
    apply_lanes(adj, l2, u[0])
    combine(part_b, got_b, sum_b, full_b, chunk_b, 2)
    finish(full_a, chunk_a, 0)
    grads[pl.ds(3 * lanes, 2 * lanes), :] = full_a[pl.ds(0, 2 * lanes), :]
    finish(full_b, chunk_b, 2)
    grads[pl.ds(0, 3 * lanes), :] = full_b[pl.ds(0, 3 * lanes), :]


def on_device(initial_state, gate_angles, gate_pairs, hop_coef, hop_mask):
    top_local, mid_count, lanes = initial_state.shape
    blocks = gate_angles.shape[0]
    n = lax.axis_size(AXIS)
    top = top_local * n
    low = mid_count // n
    rows = top_local * mid_count
    ranks = (top // low).bit_length() - 1
    vmem = pl.BlockSpec(memory_space=pltpu.VMEM)
    smem = pl.BlockSpec(memory_space=pltpu.SMEM)
    flat = jax.ShapeDtypeStruct((rows, lanes), f32)
    gates = jax.ShapeDtypeStruct((blocks, lanes, lanes), f32)
    s0 = initial_state.reshape(rows, lanes)
    ut, u, s1, s2, s3 = pl.pallas_call(
        functools.partial(front_kernel, mid_count),
        out_shape=[gates, gates, flat, flat, flat],
        in_specs=[smem, vmem, vmem],
        out_specs=[vmem] * 5,
        name="front",
    )(gate_pairs, s0, gate_angles)
    s3 = s3.reshape(initial_state.shape)
    chunk_a = 8 * -(-2 * lanes // (8 * n))
    chunk_b = 8 * -(-3 * lanes // (8 * n))
    bits = (low,) + (2,) * ranks + (top >> ranks, lanes)
    half = (ranks, low) + (2,) * (ranks - 1) + (top >> ranks, lanes)
    full = (rows, lanes)
    tall = (top, low, lanes)
    adjoint, grads = pl.pallas_call(
        functools.partial(main_kernel, n, mid_count, ranks),
        out_shape=[flat, jax.ShapeDtypeStruct((blocks * lanes, lanes), f32)],
        in_specs=[smem, smem] + [vmem] * 6,
        out_specs=[vmem] * 2,
        scratch_shapes=[
            pltpu.VMEM(tall, f32),
            pltpu.VMEM(full, f32),
            pltpu.VMEM(bits, f32),
            pltpu.VMEM(bits, f32),
            pltpu.VMEM(half, f32),
            pltpu.VMEM((low // 2,) + bits[1:], f32),
            pltpu.VMEM(full, f32),
            pltpu.VMEM(tall, f32),
            pltpu.VMEM(initial_state.shape, f32),
            pltpu.VMEM(full, f32),
            pltpu.VMEM((n * chunk_a, lanes), f32),
            pltpu.VMEM((n * chunk_b, lanes), f32),
            pltpu.VMEM((n, chunk_a, lanes), f32),
            pltpu.VMEM((n, chunk_b, lanes), f32),
            pltpu.VMEM((chunk_a, lanes), f32),
            pltpu.VMEM((chunk_b, lanes), f32),
            pltpu.VMEM((n * chunk_a, lanes), f32),
            pltpu.VMEM((n * chunk_b, lanes), f32),
            pltpu.SemaphoreType.DMA((2,)),
            pltpu.SemaphoreType.DMA((2, ranks + 1)),
            pltpu.SemaphoreType.DMA((2,)),
            pltpu.SemaphoreType.DMA((2, 4)),
        ],
        compiler_params=pltpu.CompilerParams(collective_id=0, has_side_effects=True),
        name="main",
    )(hop_coef, hop_mask, s3, s2, s1, s0, ut, u)
    return adjoint.reshape(initial_state.shape), grads.reshape(blocks, lanes, lanes)


def solution(mesh):
    in_specs = (P(("runs", AXIS), None, None), P("runs", None), P(), P(), P())
    out_specs = (P(("runs", AXIS), None, None), P("runs", None, None))
    return jax.shard_map(
        on_device, mesh=mesh, in_specs=in_specs, out_specs=out_specs, check_vma=False
    )
```

profile of v0, /device:TPU:0, one launch (start us, length us, event | category | flops | bytes accessed | tf_op | source)
XLA Modules:
  0.0 86.1 jit_solution(15744864576198942151)
XLA Ops:
  0.6 1.4 %copy.7.pairs = s32[5,16,2]{2,1,0:T(8,128)} copy(s32[5,16,2]{1,2,0:T(2,128)} %param.7) | data formatting | bytes 1280 | tf_op args[2]
  2.0 6.4 %front.1 = (f32[5,128,128]{2,1,0:T(8,128)}, f32[5,128,128]{2,1,0:T(8,128)}, f32[1024,128]{1,0:T(8,128)}, f32[1024,128]{1,0:T(8,128)}, f32[1024,128]{1,0:T(8,128)}) custom-call(s32[5,16,2]{2,1,0:T(8,128)} %copy.7.pairs, f32[1024,128]{1,0:T(8,128)} %bitcast.4, f32[5,16]{1,0:T(8,128)} %angles.1), custom_call_target="tpu_custom_call" | custom-call | tf_op jit(solution)/shard_map/front/pallas_call | solution.py:402
  8.5 74.9 %main.1 = (f32[1024,128]{1,0:T(8,128)}, f32[640,128]{1,0:T(8,128)}) custom-call(f32[23]{0:T(128)} %coef.1, s32[23]{0:T(128)} %mask.1, f32[8,128,128]{2,1,0:T(8,128)} %bitcast.6, f32[1024,128]{1,0:T(8,128)} %get-tuple-element.10.s2, f32[1024,128]{1,0:T(8,128)} %get-tuple-element.11.s1, f32[1024,128]{1,0:T(8,128)} %bitcast.5, ...), custom_call_target="tpu_custom_call" | custom-call | tf_op jit(solution)/shard_map/main/pallas_call | solution.py:416
  83.4 0.0 copy-start
  83.4 1.9 %copy.10 = f32[8,128,128]{2,1,0:T(8,128)} copy(f32[8,128,128]{2,1,0:T(8,128)} %bitcast.7) | data formatting | bytes 1048576
  85.3 0.0 copy-done
  85.3 0.7 copy.11
Async XLA Ops:
  83.4 1.9 %copy-start = (f32[640,128]{1,0:T(8,128)S(1)}, f32[640,128]{1,0:T(8,128)}, u32[]{:S(2)}) copy-start(f32[640,128]{1,0:T(8,128)} %get-tuple-element.15) | copy-start | bytes 983044
where the time goes:
time: 86.3 us; the launch traced here: 86.1 us
  Pallas kernels  81.4 us (94%)
  local copies, waits for them, and re-layouts  4.05 us (5%)
    pallas_call x1, Pallas kernels, on_device(): pl.pallas_call(functools.partial(main_kernel, n, mid_count, ranks), out_s...  74.9 us
    pallas_call x1, Pallas kernels, on_device(): pl.pallas_call(functools.partial(front_kernel, mid_count), out_shape=[gat...  6.43 us
    unnamed x5, local copies, waits for them, and re-layouts  4.05 us

commit v1 on v0

--- a/solution.py
+++ b/solution.py
@@ -135,20 +135,18 @@
     return [g * stride * lanes + s for g in range(groups) for s in range(stride)], stride
 
 
-def front_kernel(mid_count, pairs, x, angles, ut, u, s1, s2, s3):
-    blocks, lanes = ut.shape[0], ut.shape[1]
-    givens = angles.shape[1]
-    cosines = jnp.cos(angles[...])
-    sines = jnp.sin(angles[...])
+def build_gates(pairs, cosines, sines, ut, u, which):
+    lanes = ut.shape[1]
+    givens = cosines.shape[1]
     lane = lax.broadcasted_iota(jnp.int32, (8, lanes), 1)
     row = lax.broadcasted_iota(jnp.int32, (lanes, lanes), 0)
     col = lax.broadcasted_iota(jnp.int32, (lanes, lanes), 1)
-    for b in range(blocks):
+    for b in which:
         ut[b] = jnp.where(row == col, 1.0, 0.0)
     for g in range(givens):
-        for b in range(blocks):
-            p = pairs[b, g, 0]
-            s = pairs[b, g, 1]
+        for b in which:
+            p = pairs[b, 0, g]
+            s = pairs[b, 1, g]
             low = lax.shift_right_logical(lane, p) & 1
             high = lax.shift_right_logical(lane, s) & 1
             cosine = jnp.broadcast_to(cosines[b : b + 1, g : g + 1], (8, lanes))
@@ -163,12 +161,8 @@
                 + pltpu.roll(now, (lanes - gap) & (lanes - 1), 1) * up
                 + pltpu.roll(now, (lanes + gap) & (lanes - 1), 1) * down
             )
-    for b in range(blocks):
+    for b in which:
         u[b] = jnp.transpose(ut[b])
-    apply_lanes(s1, x, ut[0])
-    apply_quads(s2, quads(s1), ut[1])
-    starts, stride = mid_starts(x.shape[0], mid_count, lanes)
-    apply_rows(s3, s2, u[2], starts, lanes, stride)
 
 
 def hop_matrix(size, terms):
@@ -192,8 +186,9 @@
 
 
 def main_kernel(
-    n, mid_count, ranks, coef, mask, s3, s2, s1, s0, ut, u,
+    n, mid_count, ranks, pairs, coef, mask, angles, s0,
     adj, grads,
+    ut, u, s1, s2, s3,
     xb, s4, yb, zb, rungs, chain, l4, l3, back, l2,
     part_a, part_b, got_a, got_b, sum_a, sum_b, full_a, full_b,
     sem_a, sem_x, sem_b, sem_r,
@@ -216,6 +211,14 @@
 
     barrier = pltpu.get_barrier_semaphore()
     each_peer(lambda peer: pl.semaphore_signal(barrier, inc=1, device_id={AXIS: peer}))
+
+    cosines = jnp.cos(angles[...])
+    sines = jnp.sin(angles[...])
+    build_gates(pairs, cosines, sines, ut, u, (0, 1, 2))
+    starts, stride = mid_starts(mid_flat, mid_count, lanes)
+    apply_lanes(s1, s0, ut[0])
+    apply_quads(s2, quads(s1), ut[1])
+    apply_rows(s3.reshape(mid_flat, lanes), s2, u[2], starts, lanes, stride)
     pl.semaphore_wait(barrier, n - 1)
 
     def remote(src, dst, send, recv, peer):
@@ -239,6 +242,7 @@
     )
     xb[mine_rows] = s3[:, mine_mid, :]
 
+    build_gates(pairs, cosines, sines, ut, u, (3, 4))
     weights = [coef[h] * mask[h].astype(f32) for h in range(coef.shape[0])]
     first_top = lane_bits + YQ
     first_rung = first_top + top_bits - 1
@@ -259,33 +263,27 @@
     apply_rows(s4f, xf, u[3], near, lanes, 1)
     u4 = split(u[4])
     inner = yb.shape[1:]
+    own_bits = [lax.rem(me // (2**k), 2) for k in range(ranks)]
+    half_low = low // 2
+
+    def half(ref, k, side):
+        where = (slice(None),) * (ranks - 1 - k) + (side,)
+        return ref.at[where]
+
+    def partner(k):
+        return me + (1 - 2 * own_bits[k]) * 2**k
+
     for c in planes:
         yb[c] = dot3(u4, s4f[pl.ds(c, top, stride=low), :]).reshape(inner)
-
-    copies = []
-    own_bits = [lax.rem(me // (2**k), 2) for k in range(ranks)]
-
-    def half(ref, k, side):
-        where = (slice(None),) * (ranks - k) + (side,)
-        return ref.at[where]
-
-    def partner(k):
-        return me + (1 - 2 * own_bits[k]) * 2**k
-
-    for k in range(ranks - 1, -1, -1):
-        copies.append(
-            remote(half(yb, k, 1 - own_bits[k]), rungs.at[k], sem_x.at[0, k], sem_x.at[1, k],
-                   partner(k))
-        )
-    half_low = low // 2
-    copies.append(
-        remote(
-            yb.at[pl.ds((1 - own_bits[0]) * half_low, half_low)], chain,
-            sem_x.at[0, ranks], sem_x.at[1, ranks], partner(0),
-        )
-    )
-    for copy in copies:
-        copy.start()
+        for k in range(ranks - 1, -1, -1):
+            remote(
+                half(yb.at[c], k, 1 - own_bits[k]), rungs.at[k, c],
+                sem_x.at[0, k], sem_x.at[1, k], partner(k),
+            ).start()
+    remote(
+        yb.at[pl.ds((1 - own_bits[0]) * half_low, half_low)], chain,
+        sem_x.at[0, ranks], sem_x.at[1, ranks], partner(0),
+    ).start()
 
     lane = lax.broadcasted_iota(jnp.int32, (top, lanes), 1)
     lane_top = lax.shift_right_logical(lane, lane_bits - 1) & 1
@@ -302,22 +300,18 @@
         total = total + jnp.where(lane_top != (c & 1), weights[lane_bits - 1] * rolled, 0.0)
         zb[c] = total.reshape(inner)
 
-    for copy in copies:
-        copy.wait()
+    seat = pl.ds((1 - own_bits[0]) * half_low, half_low)
+    settle(chain, sem_x.at[0, ranks], sem_x.at[1, ranks])
+    zb[seat] = zb[seat] + weights[lane_bits + low_bits - 1] * chain[...]
     for k in range(ranks):
-        place = half(zb, k, 1 - own_bits[k])
-        place[...] = place[...] + weights[first_rung + low_bits + k] * rungs[k]
-    seat = pl.ds((1 - own_bits[0]) * half_low, half_low)
-    zb[seat] = zb[seat] + weights[lane_bits + low_bits - 1] * chain[...]
+        settle(rungs.at[k], sem_x.at[0, k], sem_x.at[1, k])
+        for c in planes:
+            place = half(zb.at[c], k, 1 - own_bits[k])
+            place[...] = place[...] + weights[first_rung + low_bits + k] * rungs[k, c]
 
     ut4 = split(ut[4])
-    gram = None
     for c in planes:
-        lam = split(zb[c].reshape(top, lanes))
-        part = dot3(lam, s4f[pl.ds(c, top, stride=low), :], NT)
-        gram = part if gram is None else gram + part
-        l4f[pl.ds(c, top, stride=low), :] = dot3(ut4, lam)
-    part_a[pl.ds(lanes, lanes), :] = gram
+        l4f[pl.ds(c, top, stride=low), :] = dot3(ut4, zb[c].reshape(top, lanes))
     apply_rows(l3f, l4f, ut[3], near, lanes, 1)
 
     each_peer(
@@ -327,6 +321,15 @@
         ).start()
     )
     back[:, mine_mid, :] = l3[mine_rows]
+    gram = None
+    for c in range(0, low, 2):
+        lam = jnp.concatenate([zb[c + i].reshape(top, lanes) for i in range(2)], axis=1)
+        old = jnp.concatenate(
+            [s4f[pl.ds(c + i, top, stride=low), :] for i in range(2)], axis=1
+        )
+        part = dot3(lam, old, NT)
+        gram = part if gram is None else gram + part
+    part_a[pl.ds(lanes, lanes), :] = gram
     part_a[pl.ds(0, lanes), :] = gram_rows(l4f, xf, near, lanes, 1)
 
     def scatter(part, got, chunk, number):
@@ -369,7 +372,6 @@
     low_part = pl.ds(0, (n - 1) * low)
     settle(back.at[:, low_part, :], sem_b.at[0], sem_b.at[1])
     backf = back.reshape(mid_flat, lanes)
-    starts, stride = mid_starts(mid_flat, mid_count, lanes)
     part_b[pl.ds(2 * lanes, lanes), :] = gram_rows(backf, s2, starts, lanes, stride)
     apply_rows(l2, backf, ut[2], starts, lanes, stride)
     combine(part_a, got_a, sum_a, full_a, chunk_a, 0)
@@ -397,16 +399,8 @@
     vmem = pl.BlockSpec(memory_space=pltpu.VMEM)
     smem = pl.BlockSpec(memory_space=pltpu.SMEM)
     flat = jax.ShapeDtypeStruct((rows, lanes), f32)
-    gates = jax.ShapeDtypeStruct((blocks, lanes, lanes), f32)
+    gates = (blocks, lanes, lanes)
     s0 = initial_state.reshape(rows, lanes)
-    ut, u, s1, s2, s3 = pl.pallas_call(
-        functools.partial(front_kernel, mid_count),
-        out_shape=[gates, gates, flat, flat, flat],
-        in_specs=[smem, vmem, vmem],
-        out_specs=[vmem] * 5,
-        name="front",
-    )(gate_pairs, s0, gate_angles)
-    s3 = s3.reshape(initial_state.shape)
     chunk_a = 8 * -(-2 * lanes // (8 * n))
     chunk_b = 8 * -(-3 * lanes // (8 * n))
     bits = (low,) + (2,) * ranks + (top >> ranks, lanes)
@@ -416,9 +410,14 @@
     adjoint, grads = pl.pallas_call(
         functools.partial(main_kernel, n, mid_count, ranks),
         out_shape=[flat, jax.ShapeDtypeStruct((blocks * lanes, lanes), f32)],
-        in_specs=[smem, smem] + [vmem] * 6,
+        in_specs=[smem] * 3 + [vmem] * 2,
         out_specs=[vmem] * 2,
         scratch_shapes=[
+            pltpu.VMEM(gates, f32),
+            pltpu.VMEM(gates, f32),
+            pltpu.VMEM(full, f32),
+            pltpu.VMEM(full, f32),
+            pltpu.VMEM(initial_state.shape, f32),
             pltpu.VMEM(tall, f32),
             pltpu.VMEM(full, f32),
             pltpu.VMEM(bits, f32),
@@ -444,7 +443,7 @@
         ],
         compiler_params=pltpu.CompilerParams(collective_id=0, has_side_effects=True),
         name="main",
-    )(hop_coef, hop_mask, s3, s2, s1, s0, ut, u)
+    )(jnp.transpose(gate_pairs, (0, 2, 1)), hop_coef, hop_mask, gate_angles, s0)
     return adjoint.reshape(initial_state.shape), grads.reshape(blocks, lanes, lanes)
 
 

time: 86.3 us -> 69.6 us (0.81)
  Pallas kernels: 81.4 us -> 66.2 us
  local copies, waits for them, and re-layouts: 4.05 us -> 2.65 us
    pallas_call x1, Pallas kernels: 74.9 us -> 66.2 us  [on_device(): pl.pallas_call(functools.partial(main_kernel, n, mid_count, ranks), out_s...]
    pallas_call x1 -> x0, Pallas kernels: 6.43 us -> none  [on_device(): pl.pallas_call(functools.partial(front_kernel, mid_count), out_shape=[gat...]
    unnamed x5 -> x4, local copies, waits for them, and re-layouts: 4.05 us -> 2.65 us
where the time goes in v1:
time: 69.6 us; the launch traced here: 69.5 us
  Pallas kernels  66.2 us (95%)
  local copies, waits for them, and re-layouts  2.65 us (4%)
    pallas_call x1, Pallas kernels, on_device(): pl.pallas_call(functools.partial(main_kernel, n, mid_count, ranks), out_s...  66.2 us
    unnamed x4, local copies, waits for them, and re-layouts  2.65 us

profile of v1, /device:TPU:0, one launch (start us, length us, event | category | flops | bytes accessed | tf_op | source)
XLA Modules:
  0.0 69.5 jit_solution(10058388326612807045)
XLA Ops:
  0.6 66.2 %main.1 = (f32[1024,128]{1,0:T(8,128)}, f32[640,128]{1,0:T(8,128)}) custom-call(s32[5,2,16]{2,1,0:T(2,128)} %bitcast.7, f32[23]{0:T(128)} %coef.1, s32[23]{0:T(128)} %mask.1, f32[5,16]{1,0:T(8,128)} %angles.1, f32[1024,128]{1,0:T(8,128)} %bitcast.4), custom_call_target="tpu_custom_call" | custom-call | tf_op jit(solution)/shard_map/main/pallas_call | solution.py:410
  66.8 0.0 copy-start
  66.8 1.9 %copy.9 = f32[8,128,128]{2,1,0:T(8,128)} copy(f32[8,128,128]{2,1,0:T(8,128)} %bitcast.5) | data formatting | bytes 1048576
  68.7 0.0 copy-done
  68.7 0.7 %copy.10 = f32[5,128,128]{2,1,0:T(8,128)} copy(f32[5,128,128]{2,1,0:T(8,128)S(1)} %bitcast.6) | data formatting | bytes 655360
Async XLA Ops:
  66.8 1.9 %copy-start = (f32[640,128]{1,0:T(8,128)S(1)}, f32[640,128]{1,0:T(8,128)}, u32[]{:S(2)}) copy-start(f32[640,128]{1,0:T(8,128)} %get-tuple-element.5) | copy-start | bytes 983044

commit v2 on v1

--- a/solution.py
+++ b/solution.py
@@ -190,7 +190,7 @@
     adj, grads,
     ut, u, s1, s2, s3,
     xb, s4, yb, zb, rungs, chain, l4, l3, back, l2,
-    part_a, part_b, got_a, got_b, sum_a, sum_b, full_a, full_b,
+    part_a, part_b, lent_a, lent_b, got_a, got_b, sum_a, sum_b, full_a, full_b,
     sem_a, sem_x, sem_b, sem_r,
 ):
     me = lax.axis_index(AXIS)
@@ -332,30 +332,63 @@
     part_a[pl.ds(lanes, lanes), :] = gram
     part_a[pl.ds(0, lanes), :] = gram_rows(l4f, xf, near, lanes, 1)
 
-    def scatter(part, got, chunk, number):
-        each_peer(
+    factor = 2.0 / (top * mid_count)
+    mate = partner(0)
+    pairs_of = n // 2
+
+    def each_twin(body):
+        def step(d, carry):
+            body(lax.rem(me + 2 * d, n))
+            return carry
+        lax.fori_loop(1, pairs_of, step, 0)
+
+    def own_half(chunk, side):
+        size = pairs_of * chunk
+        return pl.ds(pl.multiple_of(side * size, 8), size)
+
+    def lend(part, lent, chunk, number):
+        remote(
+            part.at[own_half(chunk, 1 - own_bits[0])], lent,
+            sem_r.at[0, number], sem_r.at[1, number], mate,
+        ).start()
+
+    def scatter(part, lent, got, chunk, number):
+        settle(lent, sem_r.at[0, number], sem_r.at[1, number])
+        lent[...] = lent[...] + part[own_half(chunk, own_bits[0]), :]
+        each_twin(
             lambda peer: remote(
-                part.at[pl.ds(pl.multiple_of(peer * chunk, 8), chunk)], got.at[me],
-                sem_r.at[0, number], sem_r.at[1, number], peer,
+                lent.at[pl.ds(pl.multiple_of(peer // 2 * chunk, 8), chunk)], got.at[me // 2],
+                sem_r.at[0, number + 1], sem_r.at[1, number + 1], peer,
             ).start()
         )
-        got[me] = part[pl.ds(pl.multiple_of(me * chunk, 8), chunk), :]
-
-    factor = 2.0 / (top * mid_count)
-
-    def combine(part, got, mine, full, chunk, number):
-        settle(got.at[pl.ds(0, n - 1)], sem_r.at[0, number], sem_r.at[1, number])
+        got[me // 2] = lent[pl.ds(pl.multiple_of(me // 2 * chunk, 8), chunk), :]
+
+    def combine(got, mine, full, chunk, number):
+        settle(got.at[pl.ds(0, pairs_of - 1)], sem_r.at[0, number + 1], sem_r.at[1, number + 1])
         mine[...] = factor * jnp.sum(got[...], axis=0)
-        spot = pl.ds(pl.multiple_of(me * chunk, 8), chunk)
-        each_peer(
+        spot = pl.ds(
+            pl.multiple_of(own_bits[0] * pairs_of * chunk + me // 2 * chunk, 8), chunk
+        )
+        each_twin(
             lambda peer: remote(
-                mine, full.at[spot], sem_r.at[0, number + 1], sem_r.at[1, number + 1], peer
+                mine, full.at[spot], sem_r.at[0, number + 2], sem_r.at[1, number + 2], peer
             ).start()
         )
         full[spot, :] = mine[...]
 
+    def trade(full, chunk, number):
+        settle(
+            full.at[pl.ds(0, (pairs_of - 1) * chunk)],
+            sem_r.at[0, number + 2], sem_r.at[1, number + 2],
+        )
+        whole = full.at[own_half(chunk, own_bits[0])]
+        remote(whole, whole, sem_r.at[0, number + 3], sem_r.at[1, number + 3], mate).start()
+
     def finish(full, chunk, number):
-        settle(full.at[pl.ds(0, (n - 1) * chunk)], sem_r.at[0, number + 1], sem_r.at[1, number + 1])
+        settle(
+            full.at[pl.ds(0, pairs_of * chunk)],
+            sem_r.at[0, number + 3], sem_r.at[1, number + 3],
+        )
 
     chunk_a = sum_a.shape[0]
     chunk_b = sum_b.shape[0]
@@ -367,24 +400,28 @@
         part_b[pl.ds(3 * lanes, n * chunk_b - 3 * lanes), :] = jnp.zeros(
             (n * chunk_b - 3 * lanes, lanes), f32
         )
-    scatter(part_a, got_a, chunk_a, 0)
+    lend(part_a, lent_a, chunk_a, 0)
+    scatter(part_a, lent_a, got_a, chunk_a, 0)
 
     low_part = pl.ds(0, (n - 1) * low)
     settle(back.at[:, low_part, :], sem_b.at[0], sem_b.at[1])
     backf = back.reshape(mid_flat, lanes)
+    apply_rows(l2, backf, ut[2], starts, lanes, stride)
     part_b[pl.ds(2 * lanes, lanes), :] = gram_rows(backf, s2, starts, lanes, stride)
-    apply_rows(l2, backf, ut[2], starts, lanes, stride)
-    combine(part_a, got_a, sum_a, full_a, chunk_a, 0)
+    combine(got_a, sum_a, full_a, chunk_a, 0)
     wide = split(quads(l2))
     part_b[pl.ds(lanes, lanes), :] = gram_quads(wide, split(quads(s1)))
     apply_quads(l2, wide, u[1])
     part_b[pl.ds(0, lanes), :] = gram_lanes(l2, s0)
-    scatter(part_b, got_b, chunk_b, 2)
+    lend(part_b, lent_b, chunk_b, 4)
+    trade(full_a, chunk_a, 0)
+    scatter(part_b, lent_b, got_b, chunk_b, 4)
     apply_lanes(adj, l2, u[0])
-    combine(part_b, got_b, sum_b, full_b, chunk_b, 2)
     finish(full_a, chunk_a, 0)
     grads[pl.ds(3 * lanes, 2 * lanes), :] = full_a[pl.ds(0, 2 * lanes), :]
-    finish(full_b, chunk_b, 2)
+    combine(got_b, sum_b, full_b, chunk_b, 4)
+    trade(full_b, chunk_b, 4)
+    finish(full_b, chunk_b, 4)
     grads[pl.ds(0, 3 * lanes), :] = full_b[pl.ds(0, 3 * lanes), :]
 
 
@@ -430,8 +467,10 @@
             pltpu.VMEM(full, f32),
             pltpu.VMEM((n * chunk_a, lanes), f32),
             pltpu.VMEM((n * chunk_b, lanes), f32),
-            pltpu.VMEM((n, chunk_a, lanes), f32),
-            pltpu.VMEM((n, chunk_b, lanes), f32),
+            pltpu.VMEM((n // 2 * chunk_a, lanes), f32),
+            pltpu.VMEM((n // 2 * chunk_b, lanes), f32),
+            pltpu.VMEM((n // 2, chunk_a, lanes), f32),
+            pltpu.VMEM((n // 2, chunk_b, lanes), f32),
             pltpu.VMEM((chunk_a, lanes), f32),
             pltpu.VMEM((chunk_b, lanes), f32),
             pltpu.VMEM((n * chunk_a, lanes), f32),
@@ -439,7 +478,7 @@
             pltpu.SemaphoreType.DMA((2,)),
             pltpu.SemaphoreType.DMA((2, ranks + 1)),
             pltpu.SemaphoreType.DMA((2,)),
-            pltpu.SemaphoreType.DMA((2, 4)),
+            pltpu.SemaphoreType.DMA((2, 8)),
         ],
         compiler_params=pltpu.CompilerParams(collective_id=0, has_side_effects=True),
         name="main",

time: 69.6 us -> 68.3 us (0.981)
  Pallas kernels: 66.2 us -> 64.9 us
    pallas_call x1, Pallas kernels: 66.2 us -> 64.9 us  [on_device(): pl.pallas_call(functools.partial(main_kernel, n, mid_count, ranks), out_s...]
where the time goes in v2:
time: 68.3 us; the launch traced here: 68.2 us
  Pallas kernels  64.9 us (95%)
  local copies, waits for them, and re-layouts  2.65 us (4%)
    pallas_call x1, Pallas kernels, on_device(): pl.pallas_call(functools.partial(main_kernel, n, mid_count, ranks), out_s...  64.9 us
    unnamed x4, local copies, waits for them, and re-layouts  2.65 us

profile of v2, /device:TPU:0, one launch (start us, length us, event | category | flops | bytes accessed | tf_op | source)
XLA Modules:
  0.0 68.2 jit_solution(14825072420116147734)
XLA Ops:
  0.6 64.9 %main.1 = (f32[1024,128]{1,0:T(8,128)}, f32[640,128]{1,0:T(8,128)}) custom-call(s32[5,2,16]{2,1,0:T(2,128)} %bitcast.7, f32[23]{0:T(128)} %coef.1, s32[23]{0:T(128)} %mask.1, f32[5,16]{1,0:T(8,128)} %angles.1, f32[1024,128]{1,0:T(8,128)} %bitcast.4), custom_call_target="tpu_custom_call" | custom-call | tf_op jit(solution)/shard_map/main/pallas_call | solution.py:447
  65.5 0.0 copy-start
  65.5 1.9 %copy.9 = f32[8,128,128]{2,1,0:T(8,128)} copy(f32[8,128,128]{2,1,0:T(8,128)} %bitcast.5) | data formatting | bytes 1048576
  67.4 0.0 copy-done
  67.4 0.7 %copy.10 = f32[5,128,128]{2,1,0:T(8,128)} copy(f32[5,128,128]{2,1,0:T(8,128)S(1)} %bitcast.6) | data formatting | bytes 655360
Async XLA Ops:
  65.5 1.9 %copy-start = (f32[640,128]{1,0:T(8,128)S(1)}, f32[640,128]{1,0:T(8,128)}, u32[]{:S(2)}) copy-start(f32[640,128]{1,0:T(8,128)} %get-tuple-element.5) | copy-start | bytes 983044

commit v3 on v2

--- a/solution.py
+++ b/solution.py
@@ -329,8 +329,8 @@
         )
         part = dot3(lam, old, NT)
         gram = part if gram is None else gram + part
-    part_a[pl.ds(lanes, lanes), :] = gram
-    part_a[pl.ds(0, lanes), :] = gram_rows(l4f, xf, near, lanes, 1)
+    part_a[pl.ds(2 * lanes, lanes), :] = gram
+    part_a[pl.ds(lanes, lanes), :] = gram_rows(l4f, xf, near, lanes, 1)
 
     factor = 2.0 / (top * mid_count)
     mate = partner(0)
@@ -392,37 +392,32 @@
 
     chunk_a = sum_a.shape[0]
     chunk_b = sum_b.shape[0]
-    if n * chunk_a > 2 * lanes:
-        part_a[pl.ds(2 * lanes, n * chunk_a - 2 * lanes), :] = jnp.zeros(
-            (n * chunk_a - 2 * lanes, lanes), f32
-        )
-    if n * chunk_b > 3 * lanes:
-        part_b[pl.ds(3 * lanes, n * chunk_b - 3 * lanes), :] = jnp.zeros(
-            (n * chunk_b - 3 * lanes, lanes), f32
-        )
-    lend(part_a, lent_a, chunk_a, 0)
-    scatter(part_a, lent_a, got_a, chunk_a, 0)
-
+    for part, chunk, count in ((part_a, chunk_a, 3), (part_b, chunk_b, 2)):
+        spare = n * chunk - count * lanes
+        if spare > 0:
+            part[pl.ds(count * lanes, spare), :] = jnp.zeros((spare, lanes), f32)
     low_part = pl.ds(0, (n - 1) * low)
     settle(back.at[:, low_part, :], sem_b.at[0], sem_b.at[1])
     backf = back.reshape(mid_flat, lanes)
+    part_a[pl.ds(0, lanes), :] = gram_rows(backf, s2, starts, lanes, stride)
+    lend(part_a, lent_a, chunk_a, 0)
     apply_rows(l2, backf, ut[2], starts, lanes, stride)
-    part_b[pl.ds(2 * lanes, lanes), :] = gram_rows(backf, s2, starts, lanes, stride)
-    combine(got_a, sum_a, full_a, chunk_a, 0)
     wide = split(quads(l2))
+    apply_quads(l2, wide, u[1])
+    scatter(part_a, lent_a, got_a, chunk_a, 0)
     part_b[pl.ds(lanes, lanes), :] = gram_quads(wide, split(quads(s1)))
-    apply_quads(l2, wide, u[1])
     part_b[pl.ds(0, lanes), :] = gram_lanes(l2, s0)
     lend(part_b, lent_b, chunk_b, 4)
+    scatter(part_b, lent_b, got_b, chunk_b, 4)
+    combine(got_a, sum_a, full_a, chunk_a, 0)
+    apply_lanes(adj, l2, u[0])
+    combine(got_b, sum_b, full_b, chunk_b, 4)
     trade(full_a, chunk_a, 0)
-    scatter(part_b, lent_b, got_b, chunk_b, 4)
-    apply_lanes(adj, l2, u[0])
+    trade(full_b, chunk_b, 4)
     finish(full_a, chunk_a, 0)
-    grads[pl.ds(3 * lanes, 2 * lanes), :] = full_a[pl.ds(0, 2 * lanes), :]
-    combine(got_b, sum_b, full_b, chunk_b, 4)
-    trade(full_b, chunk_b, 4)
+    grads[pl.ds(2 * lanes, 3 * lanes), :] = full_a[pl.ds(0, 3 * lanes), :]
     finish(full_b, chunk_b, 4)
-    grads[pl.ds(0, 3 * lanes), :] = full_b[pl.ds(0, 3 * lanes), :]
+    grads[pl.ds(0, 2 * lanes), :] = full_b[pl.ds(0, 2 * lanes), :]
 
 
 def on_device(initial_state, gate_angles, gate_pairs, hop_coef, hop_mask):
@@ -438,8 +433,8 @@
     flat = jax.ShapeDtypeStruct((rows, lanes), f32)
     gates = (blocks, lanes, lanes)
     s0 = initial_state.reshape(rows, lanes)
-    chunk_a = 8 * -(-2 * lanes // (8 * n))
-    chunk_b = 8 * -(-3 * lanes // (8 * n))
+    chunk_a = 8 * -(-3 * lanes // (8 * n))
+    chunk_b = 8 * -(-2 * lanes // (8 * n))
     bits = (low,) + (2,) * ranks + (top >> ranks, lanes)
     half = (ranks, low) + (2,) * (ranks - 1) + (top >> ranks, lanes)
     full = (rows, lanes)

time: 68.3 us -> 66.6 us (0.975)
  Pallas kernels: 64.9 us -> 63.1 us
    pallas_call x1, Pallas kernels: 64.9 us -> 63.1 us  [on_device(): pl.pallas_call(functools.partial(main_kernel, n, mid_count, ranks), out_s...]
where the time goes in v3:
time: 66.6 us; the launch traced here: 66.4 us
  Pallas kernels  63.1 us (95%)
  local copies, waits for them, and re-layouts  2.65 us (4%)
    pallas_call x1, Pallas kernels, on_device(): pl.pallas_call(functools.partial(main_kernel, n, mid_count, ranks), out_s...  63.1 us
    unnamed x4, local copies, waits for them, and re-layouts  2.65 us

profile of v3, /device:TPU:0, one launch (start us, length us, event | category | flops | bytes accessed | tf_op | source)
XLA Modules:
  0.0 66.4 jit_solution(5460131303997939771)
XLA Ops:
  0.6 63.1 %main.1 = (f32[1024,128]{1,0:T(8,128)}, f32[640,128]{1,0:T(8,128)}) custom-call(s32[5,2,16]{2,1,0:T(2,128)} %bitcast.7, f32[23]{0:T(128)} %coef.1, s32[23]{0:T(128)} %mask.1, f32[5,16]{1,0:T(8,128)} %angles.1, f32[1024,128]{1,0:T(8,128)} %bitcast.4), custom_call_target="tpu_custom_call" | custom-call | tf_op jit(solution)/shard_map/main/pallas_call | solution.py:442
  63.7 0.0 copy-start
  63.8 1.9 %copy.9 = f32[8,128,128]{2,1,0:T(8,128)} copy(f32[8,128,128]{2,1,0:T(8,128)} %bitcast.5) | data formatting | bytes 1048576
  65.7 0.0 copy-done
  65.7 0.7 %copy.10 = f32[5,128,128]{2,1,0:T(8,128)} copy(f32[5,128,128]{2,1,0:T(8,128)S(1)} %bitcast.6) | data formatting | bytes 655360
Async XLA Ops:
  63.7 1.9 %copy-start = (f32[640,128]{1,0:T(8,128)S(1)}, f32[640,128]{1,0:T(8,128)}, u32[]{:S(2)}) copy-start(f32[640,128]{1,0:T(8,128)} %get-tuple-element.5) | copy-start | bytes 983044
